TPU v7x, 512 devices: a whole 4x4x16 slice. The times are simulated.
512 devices in a mesh: dp: 16 (over x_hi, y, core), tensor: 32 (over z, x_lo).
Axes of the slice: x: 4 (x_hi: 2, x_lo: 2; x = x_hi * 2 + x_lo), y: 4, z: 16, core: 2. Of those that a mesh axis runs over, the one named last changes fastest.
Arguments:
- features: bfloat16 [8192, 16384], P('tensor', 'dp'), may hold values from -6 to 6
- up_blocks: bfloat16 [64, 128, 512], P('tensor', 'dp'), may hold values from -0.5 to 0.5
- down_blocks: bfloat16 [64, 512, 128], P('tensor', 'dp'), may hold values from -0.25 to 0.25
- out_cotangent: bfloat16 [8192, 16384], P('tensor', 'dp'), may hold values from -6 to 6
Outputs:
- mixed: bfloat16 [8192, 16384], P('tensor', 'dp')
- feature_grad: bfloat16 [8192, 16384], P('tensor', 'dp')
- up_grad: float32 [64, 128, 512], P('tensor', 'dp')
- down_grad: float32 [64, 512, 128], P('tensor', 'dp')
All inputs are finite; a program needn't handle non-finite values.
Results may differ from a plain program's by a relative error of at most 0.023.
Values may be sent and summed in bfloat16 or wider, within the bound.
No kernel may reach another device: no remote copies, remote signals or barrier semaphores. Data moves between devices by JAX's collectives and lax.ppermute only.
A program may use at most 64 MiB of HBM per device.

v0:
```python
import jax
import jax.numpy as jnp
from jax import lax
from jax.sharding import PartitionSpec as P

NB = 64
BIN = 128
BOUT = 512
J_UP = 8
J_DN = 2


def gelu_value(v):
    return 0.5 * v * (1.0 + lax.erf(v * 0.7071067811865476))


def gelu_slope(v):
    return (
        0.5 * (1.0 + lax.erf(v * 0.7071067811865476))
        + v * jnp.exp(-0.5 * v * v) * 0.3989422804014327
    )


def per_device(features, up_blocks, down_blocks, out_cotangent):
    local_blocks = up_blocks.shape[0]
    tok_local = features.shape[1]
    dp_count = lax.axis_size("dp")
    x_local = features.reshape(local_blocks, BIN, tok_local)
    down_whole = lax.all_gather(down_blocks, "dp", axis=1, tiled=True)
    down_four = down_whole.reshape(local_blocks, BOUT, NB, J_DN)
    piece = lax.all_gather(up_blocks, "dp", axis=1, tiled=True)
    rows_now = piece.shape[1]
    x_rows = x_local
    pre_sum = jnp.einsum(
        "bkgj,bkt->gbjt",
        piece.reshape(local_blocks, rows_now, NB, J_UP),
        x_rows,
        preferred_element_type=jnp.float32,
    )
    pre = pre_sum.astype(jnp.bfloat16)
    received = lax.all_to_all(pre, "tensor", split_axis=0, concat_axis=1, tiled=True)
    items = received.shape[3]
    permuted = received.reshape(local_blocks, BOUT, items)
    hidden_act = gelu_value(permuted.astype(jnp.float32)).astype(jnp.bfloat16)
    blockout = jnp.einsum(
        "gmt,gmbj->bgjt", hidden_act, down_four, preferred_element_type=jnp.float32
    ).astype(jnp.bfloat16)
    returned = lax.all_to_all(blockout, "tensor", split_axis=0, concat_axis=1, tiled=True)
    permuted, act, mixed_blocks = (permuted, hidden_act, returned.reshape(local_blocks, BIN, items))
    mixed = mixed_blocks.reshape(local_blocks * BIN, tok_local)
    shaped = out_cotangent.reshape(local_blocks, NB, J_DN, tok_local)
    dblock = lax.all_to_all(shaped, "tensor", split_axis=1, concat_axis=0, tiled=True)
    dact = jnp.einsum("gmbj,bgjt->gmt", down_four, dblock, preferred_element_type=jnp.float32)
    dperm = (dact * gelu_slope(permuted.astype(jnp.float32))).astype(jnp.bfloat16)
    term = jnp.einsum("gmt,bgjt->mgbj", act, dblock, preferred_element_type=jnp.float32)
    down_share = lax.psum_scatter(
        term.reshape(BOUT // dp_count * lax.axis_size("dp"), local_blocks, BIN).astype(
            jnp.bfloat16
        ),
        "dp",
        scatter_dimension=0,
        tiled=True,
    ).astype(jnp.float32)
    down_grad = down_share.transpose(1, 0, 2)
    dpre = lax.all_to_all(
        dperm.reshape(local_blocks, NB, J_UP, tok_local),
        "tensor",
        split_axis=1,
        concat_axis=0,
        tiled=True,
    )
    x_rows = x_local
    term = jnp.einsum("bkt,gbjt->kbgj", x_rows, dpre, preferred_element_type=jnp.float32)
    up_share = lax.psum_scatter(
        term.reshape(BIN // dp_count * lax.axis_size("dp"), local_blocks, BOUT).astype(
            jnp.bfloat16
        ),
        "dp",
        scatter_dimension=0,
        tiled=True,
    ).astype(jnp.float32)
    up_grad = up_share.transpose(1, 0, 2)
    piece = lax.all_gather(up_blocks, "dp", axis=1, tiled=True)
    rows_now = piece.shape[1]
    fgrad = jnp.einsum(
        "bkgj,gbjt->bkt",
        piece.reshape(local_blocks, rows_now, NB, J_UP),
        dpre,
        preferred_element_type=jnp.float32,
    ).astype(jnp.bfloat16)
    feature_grad = fgrad.reshape(local_blocks * BIN, tok_local)
    return (mixed, feature_grad, up_grad, down_grad)


def solution(mesh):
    placed = (
        P("tensor", "dp"),
        P("tensor", "dp", None),
        P("tensor", "dp", None),
        P("tensor", "dp"),
    )
    return jax.shard_map(
        per_device,
        mesh=mesh,
        in_specs=placed,
        out_specs=(
            P("tensor", "dp"),
            P("tensor", "dp"),
            P("tensor", "dp", None),
            P("tensor", "dp", None),
        ),
        check_vma=False,
    )
```

profile of v0, /device:TPU:32, one launch (start us, length us, event | category | flops | bytes accessed | tf_op | source)
XLA Modules:
  0.0 538.5 jit_solution(7308746396229365794)
XLA Ops:
  7.2 0.0 copy-start
  7.2 1.3 reshape.41
  8.5 1.2 copy.54
  9.6 16.3 %all-to-all-start.2 = ((bf16[2,64,2,1024]{3,2,0,1:T(2,128)(2,1)}), bf16[2,64,2,1024]{3,2,0,1:T(2,128)(2,1)S(1)}, u32[]{:S(2)}, u32[]{:S(2)}) async-start(bf16[2,64,2,1024]{3,2,0,1:T(2,128)(2,1)} %copy.54), calls=%async_computation.2 | async-start | bytes 1048576 | tf_op jit(solution)/shard_map/all_to_all | solution.py:52
  25.9 0.7 copy.45
  26.7 25.2 %all_gather.7 = bf16[2,128,512]{2,0,1:T(2,128)(2,1)S(1)} all-gather(bf16[2,8,512]{2,0,1:T(2,128)(2,1)S(1)} %copy.45), channel_id=1, replica_groups=mesh['dp'=16,'tensor'=32] {'dp'}, dimensions={1}, use_global_device_ids=true | all-gather | bytes 278528 | tf_op jit(solution)/shard_map/all_gather | solution.py:31
  51.9 0.2 copy.46
  52.1 0.0 copy-done
  52.1 0.7 convert_bitcast_fusion
  52.8 0.0 copy-start.4
  52.8 2.5 copy.48
  55.3 2.0 all-to-all-done.2
  57.4 10.2 %all-to-all-start = ((bf16[64,2,8,1024]{3,2,1,0:T(8,128)(2,1)}), bf16[64,2,8,1024]{3,2,1,0:T(8,128)(2,1)S(1)}, u32[]{:S(2)}, u32[]{:S(2)}) async-start(bf16[64,2,8,1024]{3,2,1,0:T(8,128)(2,1)} %copy.48), calls=%async_computation | async-start | bytes 4194304 | tf_op jit(solution)/shard_map/all_to_all | solution.py:41
  67.6 0.0 copy-done.4
  67.6 22.2 %all_gather.8 = bf16[2,512,128]{2,1,0:T(8,128)(2,1)} all-gather(bf16[2,32,128]{2,1,0:T(8,128)(2,1)S(1)} %copy-done.4), channel_id=1, replica_groups=mesh['dp'=16,'tensor'=32] {'dp'}, dimensions={1}, use_global_device_ids=true | all-gather | bytes 278528 | tf_op jit(solution)/shard_map/all_gather | solution.py:29
  89.8 1.8 copy.50
  91.7 1.2 copy.56
  92.9 1.2 all_to_all.51
  94.1 0.0 copy-start.1
  94.1 73.4 %all-to-all-done = bf16[64,2,8,1024]{3,2,1,0:T(8,128)(2,1)S(1)} async-done(((bf16[64,2,8,1024]{3,2,1,0:T(8,128)(2,1)}), bf16[64,2,8,1024]{3,2,1,0:T(8,128)(2,1)S(1)}, u32[]{:S(2)}, u32[]{:S(2)}) %all-to-all-start) | async-done | bytes 2097184 | tf_op jit(solution)/shard_map/all_to_all | solution.py:41
  167.5 0.5 copy.49
  168.0 0.0 copy-start.2
  168.0 1.2 fusion.7
  169.2 0.0 copy-done.1
  169.2 0.0 copy-done.2
  169.2 1.5 fusion.14
  170.7 0.0 copy-start.3
  170.7 1.6 copy.58
  172.3 4.6 all-to-all-start.3
  176.8 0.0 copy-done.3
  176.8 0.5 fusion.19
  177.3 1.3 copy.52
  178.6 97.2 %all-to-all-done.3 = bf16[2,64,8,1024]{3,2,0,1:T(8,128)(2,1)} async-done(((bf16[2,64,8,1024]{3,2,0,1:T(8,128)(2,1)}), bf16[2,64,8,1024]{3,2,0,1:T(8,128)(2,1)}, u32[]{:S(2)}, u32[]{:S(2)}) %all-to-all-start.3) | async-done | bytes 2097184 | tf_op jit(solution)/shard_map/all_to_all | solution.py:65
  275.8 4.4 all-to-all-start.1
  280.2 0.0 all-reduce.3.cloned.1.call-start
  280.3 1.3 dynamic-slice
  282.2 1.9 fusion.26
  284.1 0.3 copy.63
  284.3 1.0 copy.64
  285.4 0.0 all-reduce.3.cloned.1.call-update
  285.4 0.2 reduce-scatter.4.cloned.1.call-start
  285.6 5.1 copy.84
  290.7 2.7 all_to_all.55
  293.5 0.7 fusion.25
  294.2 0.9 copy.61
  295.1 1.8 copy.74
  296.9 0.0 reduce-scatter.4.cloned.1.call-update
  296.9 138.8 %all-reduce.3.cloned.1.call-done = bf16[512,2,128]{2,1,0:T(2,128)(2,1)} async-done(((bf16[512,2,128]{2,1,0:T(2,128)(2,1)}), bf16[512,2,128]{2,1,0:T(2,128)(2,1)}) %all-reduce.3.cloned.1.call-update) | async-done | bytes 262160
  435.7 0.7 convert_bitcast_fusion.1
  436.5 0.6 copy.65
  437.1 0.0 all-to-all-done.1
  437.1 1.2 copy.53
  438.2 2.0 reshape_reshape.3
  440.3 1.3 fusion.15
  441.6 88.8 %reduce-scatter.4.cloned.1.call-done = bf16[8,1024]{1,0:T(8,128)(2,1)} async-done(((bf16[128,1024]{1,0:T(8,128)(2,1)}), bf16[8,1024]{1,0:T(8,128)(2,1)}) %reduce-scatter.4.cloned.1.call-update) | async-done | bytes 16400
  530.4 1.3 convert_bitcast_fusion.2
Async XLA Ops:
  7.2 44.9 %copy-start = (bf16[256,1024]{1,0:T(8,128)(2,1)S(1)}, bf16[256,1024]{1,0:T(8,128)(2,1)}, u32[]{:S(2)}) copy-start(bf16[256,1024]{1,0:T(8,128)(2,1)} %param.4) | copy-start | bytes 1572868
  9.6 47.7 %all-to-all-start.2 = ((bf16[2,64,2,1024]{3,2,0,1:T(2,128)(2,1)}), bf16[2,64,2,1024]{3,2,0,1:T(2,128)(2,1)S(1)}, u32[]{:S(2)}, u32[]{:S(2)}) async-start(bf16[2,64,2,1024]{3,2,0,1:T(2,128)(2,1)} %copy.54), calls=%async_computation.2 | async-start | bytes 1048576 | tf_op jit(solution)/shard_map/all_to_all | solution.py:52
  52.8 14.8 %copy-start.4 = (bf16[2,32,128]{2,1,0:T(8,128)(2,1)S(1)}, bf16[2,32,128]{2,1,0:T(8,128)(2,1)}, u32[]{:S(2)}) copy-start(bf16[2,32,128]{2,1,0:T(8,128)(2,1)} %param.6) | copy-start | bytes 49156
  57.4 110.1 %all-to-all-start = ((bf16[64,2,8,1024]{3,2,1,0:T(8,128)(2,1)}), bf16[64,2,8,1024]{3,2,1,0:T(8,128)(2,1)S(1)}, u32[]{:S(2)}, u32[]{:S(2)}) async-start(bf16[64,2,8,1024]{3,2,1,0:T(8,128)(2,1)} %copy.48), calls=%async_computation | async-start | bytes 4194304 | tf_op jit(solution)/shard_map/all_to_all | solution.py:41
  94.1 75.0 %copy-start.1 = (bf16[64,2,2,1024]{3,0,2,1:T(8,128)(2,1)}, bf16[64,2,2,1024]{3,0,2,1:T(8,128)(2,1)S(1)}, u32[]{:S(2)}) copy-start(bf16[64,2,2,1024]{3,0,2,1:T(8,128)(2,1)S(1)} %all_to_all.51) | copy-start | bytes 1572868
  168.0 1.2 copy-start.2
  170.7 6.1 %copy-start.3 = (bf16[2,512,128]{1,0,2:T(2,128)(2,1)S(1)}, bf16[2,512,128]{1,0,2:T(2,128)(2,1)}, u32[]{:S(2)}) copy-start(bf16[2,512,128]{1,0,2:T(2,128)(2,1)} %copy.50) | copy-start | bytes 786436
  172.3 103.5 %all-to-all-start.3 = ((bf16[2,64,8,1024]{3,2,0,1:T(8,128)(2,1)}), bf16[2,64,8,1024]{3,2,0,1:T(8,128)(2,1)}, u32[]{:S(2)}, u32[]{:S(2)}) async-start(bf16[2,64,8,1024]{3,2,0,1:T(8,128)(2,1)} %copy.58), calls=%async_computation.3 | async-start | bytes 4194304 | tf_op jit(solution)/shard_map/all_to_all | solution.py:65
  275.8 161.3 %all-to-all-start.1 = ((bf16[64,2,2,1024]{3,2,1,0:T(2,128)(2,1)}), bf16[64,2,2,1024]{3,2,1,0:T(2,128)(2,1)S(1)}, u32[]{:S(2)}, u32[]{:S(2)}) async-start(bf16[64,2,2,1024]{3,2,1,0:T(2,128)(2,1)} %copy.52), calls=%async_computation.1 | async-start | bytes 1048576 | tf_op jit(solution)/shard_map/all_to_all | solution.py:48
  280.2 155.5 %all-reduce.3.cloned.1.call-start = ((), (), s32[]{:S(2)}) async-start(), calls=%async_computation.6 | async-start | bytes 524288
  285.4 244.9 %reduce-scatter.4.cloned.1.call-start = ((), (), s32[]{:S(2)}) async-start(), calls=%async_computation.5 | async-start | bytes 278528
Sparse Core Ops, SparseCore 0:
  285.5 150.1 all-reduce.2
  440.9 89.3 reduce-scatter.3
where the time goes:
time: 539 us
  waiting for transfers between devices  400 us (74%)
  blocking collectives  47.4 us (9%)
  starting transfers between devices  35.7 us (7%)
  local copies, waits for them, and re-layouts  30.5 us (6%)
  between operations  14.9 us (3%)
  matrix products  6.54 us (1%)
    unnamed x4, waiting for transfers between devices  228 us
    all_to_all x1, waiting for transfers between devices, per_device(): lax.all_to_all(dperm.reshape(local_blocks, NB, J_UP, tok_local), 'tensor'...  97.2 us
    all_to_all x1, waiting for transfers between devices, per_device(): lax.all_to_all(pre, 'tensor', split_axis=0, concat_axis=1, tiled=True)  73.4 us
    all_gather x1, blocking collectives, per_device(): piece = lax.all_gather(up_blocks, 'dp', axis=1, tiled=True)  25.2 us
    all_gather x1, blocking collectives, per_device(): down_whole = lax.all_gather(down_blocks, 'dp', axis=1, tiled=True)  22.2 us
    all_to_all x1, starting transfers between devices, per_device(): lax.all_to_all(shaped, 'tensor', split_axis=1, concat_axis=0, tiled=True)  16.3 us
  transfers between devices with their start and end apart: 6, of which 5 were waited for; matrix products, arithmetic and copies ran while one was open for 5% of the time, Pallas kernels for 0%

commit v1 on v0

--- a/solution.py
+++ b/solution.py
@@ -28,7 +28,9 @@
     x_local = features.reshape(local_blocks, BIN, tok_local)
     down_whole = lax.all_gather(down_blocks, "dp", axis=1, tiled=True)
     down_four = down_whole.reshape(local_blocks, BOUT, NB, J_DN)
-    piece = lax.all_gather(up_blocks, "dp", axis=1, tiled=True)
+    piece = jnp.concatenate(
+        lax.all_to_all(jnp.stack([up_blocks] * lax.axis_size("dp")), "dp", 0, 0), axis=1
+    )
     rows_now = piece.shape[1]
     x_rows = x_local
     pre_sum = jnp.einsum(

time: 539 us -> 573 us (1.063)
  waiting for transfers between devices: 400 us -> 419 us
  local copies, waits for them, and re-layouts: 30.5 us -> 41.5 us
    another operation x0 -> x3, local copies, waits for them, and re-layouts: none -> 13.7 us  [the longest x2 12.2 us: per_device(): piece.reshape(local_blocks, rows_now, NB, J_UP)]
    all_to_all x1, waiting for transfers between devices: 2.03 us -> 15.6 us  [per_device(): lax.all_to_all(shaped, 'tensor', split_axis=1, concat_axis=0, tiled=True)]
    all_to_all x0 -> x1, waiting for transfers between devices: none -> 7.15 us  [per_device(): lax.all_to_all(jnp.stack([up_blocks] * lax.axis_size('dp')), 'dp', 0, 0)]
    all_to_all x0 -> x1, starting transfers between devices: none -> 7.03 us  [per_device(): lax.all_to_all(jnp.stack([up_blocks] * lax.axis_size('dp')), 'dp', 0, 0)]
  transfers between devices with their start and end apart: 6 -> 7, of which waited for: 5 -> 6; matrix products, arithmetic and copies ran while one was open for 5% -> 7% of each run, Pallas kernels for 0% -> 0%
where the time goes in v1:
time: 573 us; the launch traced here: 572 us
  waiting for transfers between devices  419 us (73%)
  blocking collectives  45.9 us (8%)
  local copies, waits for them, and re-layouts  41.5 us (7%)
  starting transfers between devices  39.1 us (7%)
  between operations  14.9 us (3%)
  matrix products  7.49 us (1%)
    unnamed x4, waiting for transfers between devices  229 us
    all_to_all x1, waiting for transfers between devices, per_device(): lax.all_to_all(dperm.reshape(local_blocks, NB, J_UP, tok_local), 'tensor'...  96.1 us
    all_to_all x1, waiting for transfers between devices, per_device(): lax.all_to_all(pre, 'tensor', split_axis=0, concat_axis=1, tiled=True)  71 us
    all_gather x1, blocking collectives, per_device(): down_whole = lax.all_gather(down_blocks, 'dp', axis=1, tiled=True)  23 us
    all_gather x1, blocking collectives, per_device(): piece = lax.all_gather(up_blocks, 'dp', axis=1, tiled=True)  22.9 us
    all_to_all x1, waiting for transfers between devices, per_device(): lax.all_to_all(shaped, 'tensor', split_axis=1, concat_axis=0, tiled=True)  15.6 us
    all_to_all x1, starting transfers between devices, per_device(): lax.all_to_all(shaped, 'tensor', split_axis=1, concat_axis=0, tiled=True)  15.4 us
    another operation x2, local copies, waits for them, and re-layouts, per_device(): piece.reshape(local_blocks, rows_now, NB, J_UP)  12.2 us
  transfers between devices with their start and end apart: 7, of which 6 were waited for; matrix products, arithmetic and copies ran while one was open for 7% of the time, Pallas kernels for 0%

profile of v1, /device:TPU:32, one launch (start us, length us, event | category | flops | bytes accessed | tf_op | source)
XLA Modules:
  0.0 571.5 jit_solution(15946319433359765933)
XLA Ops:
  7.2 0.0 copy-start
  7.2 1.5 stack.2
  8.7 7.0 %all-to-all-start = ((bf16[16,2,8,512]{3,2,1,0:T(8,128)(2,1)}), bf16[16,2,8,512]{3,2,1,0:T(8,128)(2,1)S(1)}, u32[]{:S(2)}, u32[]{:S(2)}) async-start(bf16[16,2,8,512]{3,2,1,0:T(8,128)(2,1)} %stack.2), calls=%async_computation | async-start | bytes 524288 | tf_op jit(solution)/shard_map/all_to_all | solution.py:32
  15.7 1.2 reshape.45
  17.0 1.2 copy.54
  18.1 7.2 %all-to-all-done = bf16[16,2,8,512]{3,2,1,0:T(8,128)(2,1)S(1)} async-done(((bf16[16,2,8,512]{3,2,1,0:T(8,128)(2,1)}), bf16[16,2,8,512]{3,2,1,0:T(8,128)(2,1)S(1)}, u32[]{:S(2)}, u32[]{:S(2)}) %all-to-all-start) | async-done | bytes 262176 | tf_op jit(solution)/shard_map/all_to_all | solution.py:32
  25.3 15.4 %all-to-all-start.3 = ((bf16[2,64,2,1024]{3,2,0,1:T(2,128)(2,1)}), bf16[2,64,2,1024]{3,2,0,1:T(2,128)(2,1)S(1)}, u32[]{:S(2)}, u32[]{:S(2)}) async-start(bf16[2,64,2,1024]{3,2,0,1:T(2,128)(2,1)} %copy.54), calls=%async_computation.3 | async-start | bytes 1048576 | tf_op jit(solution)/shard_map/all_to_all | solution.py:54
  40.7 5.9 %reshape_reshape.6 = bf16[2,128,64,8]{3,2,1,0:T(8,128)(2,1)} reshape(bf16[2,16,8,512]{3,2,1,0:T(8,128)(2,1)S(1)} %copy.46) | data formatting | bytes 524288 | tf_op jit(solution)/shard_map/reshape;reshape | solution.py:38
  46.6 6.3 %copy.47 = bf16[2,128,64,8]{1,2,3,0:T(8,128)(2,1)S(1)} copy(bf16[2,128,64,8]{3,2,1,0:T(8,128)(2,1)} %reshape_reshape.6) | data formatting | bytes 524288 | tf_op jit(solution)/shard_map/reshape;reshape | solution.py:38
  53.0 0.0 copy-done
  53.0 0.7 convert_bitcast_fusion
  53.7 0.0 copy-start.4
  53.7 2.5 copy.48
  56.2 15.6 %all-to-all-done.3 = bf16[2,64,2,1024]{3,2,0,1:T(2,128)(2,1)S(1)} async-done(((bf16[2,64,2,1024]{3,2,0,1:T(2,128)(2,1)}), bf16[2,64,2,1024]{3,2,0,1:T(2,128)(2,1)S(1)}, u32[]{:S(2)}, u32[]{:S(2)}) %all-to-all-start.3) | async-done | bytes 524320 | tf_op jit(solution)/shard_map/all_to_all | solution.py:54
  71.8 5.5 all-to-all-start.1
  77.3 0.0 copy-done.4
  77.3 23.0 %all_gather.6 = bf16[2,512,128]{2,1,0:T(8,128)(2,1)S(1)} all-gather(bf16[2,32,128]{2,1,0:T(8,128)(2,1)S(1)} %copy-done.4), channel_id=1, replica_groups=mesh['dp'=16,'tensor'=32] {'dp'}, dimensions={1}, use_global_device_ids=true | all-gather | bytes 278528 | tf_op jit(solution)/shard_map/all_gather | solution.py:29
  100.3 0.9 copy.50
  101.2 1.2 copy.56
  102.4 1.2 all_to_all.55
  103.6 0.0 copy-start.1
  103.6 71.0 %all-to-all-done.1 = bf16[64,2,8,1024]{3,2,1,0:T(8,128)(2,1)S(1)} async-done(((bf16[64,2,8,1024]{3,2,1,0:T(8,128)(2,1)}), bf16[64,2,8,1024]{3,2,1,0:T(8,128)(2,1)S(1)}, u32[]{:S(2)}, u32[]{:S(2)}) %all-to-all-start.1) | async-done | bytes 2097184 | tf_op jit(solution)/shard_map/all_to_all | solution.py:43
  174.6 0.5 copy.49
  175.1 0.0 copy-start.2
  175.2 1.2 fusion.7
  176.3 0.0 copy-done.1
  176.3 0.0 copy-done.2
  176.3 1.5 fusion.14
  177.9 1.6 copy.58
  179.4 0.0 copy-start.3
  179.4 5.6 all-to-all-start.4
  185.1 0.5 fusion.19
  185.5 1.3 copy.52
  186.9 96.1 %all-to-all-done.4 = bf16[2,64,8,1024]{3,2,0,1:T(8,128)(2,1)} async-done(((bf16[2,64,8,1024]{3,2,0,1:T(8,128)(2,1)}), bf16[2,64,8,1024]{3,2,0,1:T(8,128)(2,1)}, u32[]{:S(2)}, u32[]{:S(2)}) %all-to-all-start.4) | async-done | bytes 2097184 | tf_op jit(solution)/shard_map/all_to_all | solution.py:67
  283.0 5.4 all-to-all-start.2
  288.4 0.0 all-reduce.3.cloned.1.call-start
  288.5 0.0 copy-done.3
  288.5 22.9 %all_gather.7 = bf16[2,128,512]{2,0,1:T(2,128)(2,1)S(1)} all-gather(bf16[2,8,512]{2,0,1:T(2,128)(2,1)S(1)} %copy.60), channel_id=1, replica_groups=mesh['dp'=16,'tensor'=32] {'dp'}, dimensions={1}, use_global_device_ids=true | all-gather | bytes 278528 | tf_op jit(solution)/shard_map/all_gather | solution.py:85
  311.4 0.9 copy.61
  312.3 1.3 dynamic-slice
  314.3 1.9 fusion.26
  316.1 0.3 copy.65
  316.4 1.0 copy.66
  317.5 0.0 all-reduce.3.cloned.1.call-update
  317.5 0.0 reduce-scatter.4.cloned.1.call-start
  317.5 5.1 copy.84
  322.6 2.7 all_to_all.59
  325.4 0.7 fusion.25
  326.1 0.2 copy.63
  326.3 0.8 copy.76
  327.1 0.0 reduce-scatter.4.cloned.1.call-update
  327.1 141.6 %all-reduce.3.cloned.1.call-done = bf16[512,2,128]{2,1,0:T(2,128)(2,1)} async-done(((bf16[512,2,128]{2,1,0:T(2,128)(2,1)}), bf16[512,2,128]{2,1,0:T(2,128)(2,1)}) %all-reduce.3.cloned.1.call-update) | async-done | bytes 262160
  468.7 0.7 convert_bitcast_fusion.1
  469.4 0.6 copy.67
  470.1 0.0 all-to-all-done.2
  470.1 1.2 copy.53
  471.2 2.0 reshape_reshape.7
  473.3 2.2 fusion.15
  475.5 87.8 %reduce-scatter.4.cloned.1.call-done = bf16[8,1024]{1,0:T(8,128)(2,1)} async-done(((bf16[128,1024]{1,0:T(8,128)(2,1)}), bf16[8,1024]{1,0:T(8,128)(2,1)}) %reduce-scatter.4.cloned.1.call-update) | async-done | bytes 16400
  563.3 1.3 convert_bitcast_fusion.2
  (2 shorter events, 0.0 us)
Async XLA Ops:
  7.2 45.8 %copy-start = (bf16[256,1024]{1,0:T(8,128)(2,1)S(1)}, bf16[256,1024]{1,0:T(8,128)(2,1)}, u32[]{:S(2)}) copy-start(bf16[256,1024]{1,0:T(8,128)(2,1)} %param.4) | copy-start | bytes 1572868
  8.7 16.6 %all-to-all-start = ((bf16[16,2,8,512]{3,2,1,0:T(8,128)(2,1)}), bf16[16,2,8,512]{3,2,1,0:T(8,128)(2,1)S(1)}, u32[]{:S(2)}, u32[]{:S(2)}) async-start(bf16[16,2,8,512]{3,2,1,0:T(8,128)(2,1)} %stack.2), calls=%async_computation | async-start | bytes 524288 | tf_op jit(solution)/shard_map/all_to_all | solution.py:32
  25.3 46.5 %all-to-all-start.3 = ((bf16[2,64,2,1024]{3,2,0,1:T(2,128)(2,1)}), bf16[2,64,2,1024]{3,2,0,1:T(2,128)(2,1)S(1)}, u32[]{:S(2)}, u32[]{:S(2)}) async-start(bf16[2,64,2,1024]{3,2,0,1:T(2,128)(2,1)} %copy.54), calls=%async_computation.3 | async-start | bytes 1048576 | tf_op jit(solution)/shard_map/all_to_all | solution.py:54
  53.7 23.6 %copy-start.4 = (bf16[2,32,128]{2,1,0:T(8,128)(2,1)S(1)}, bf16[2,32,128]{2,1,0:T(8,128)(2,1)}, u32[]{:S(2)}) copy-start(bf16[2,32,128]{2,1,0:T(8,128)(2,1)} %param.6) | copy-start | bytes 49156
  71.8 102.9 %all-to-all-start.1 = ((bf16[64,2,8,1024]{3,2,1,0:T(8,128)(2,1)}), bf16[64,2,8,1024]{3,2,1,0:T(8,128)(2,1)S(1)}, u32[]{:S(2)}, u32[]{:S(2)}) async-start(bf16[64,2,8,1024]{3,2,1,0:T(8,128)(2,1)} %copy.48), calls=%async_computation.1 | async-start | bytes 4194304 | tf_op jit(solution)/shard_map/all_to_all | solution.py:43
  103.6 72.7 %copy-start.1 = (bf16[64,2,2,1024]{3,0,2,1:T(8,128)(2,1)}, bf16[64,2,2,1024]{3,0,2,1:T(8,128)(2,1)S(1)}, u32[]{:S(2)}) copy-start(bf16[64,2,2,1024]{3,0,2,1:T(8,128)(2,1)S(1)} %all_to_all.55) | copy-start | bytes 1572868
  175.1 1.2 copy-start.2
  179.4 109.1 %copy-start.3 = (bf16[2,8,512]{2,1,0:T(8,128)(2,1)S(1)}, bf16[2,8,512]{2,1,0:T(8,128)(2,1)}, u32[]{:S(2)}) copy-start(bf16[2,8,512]{2,1,0:T(8,128)(2,1)} %param.5) | copy-start | bytes 49156
  179.4 103.6 %all-to-all-start.4 = ((bf16[2,64,8,1024]{3,2,0,1:T(8,128)(2,1)}), bf16[2,64,8,1024]{3,2,0,1:T(8,128)(2,1)}, u32[]{:S(2)}, u32[]{:S(2)}) async-start(bf16[2,64,8,1024]{3,2,0,1:T(8,128)(2,1)} %copy.58), calls=%async_computation.4 | async-start | bytes 4194304 | tf_op jit(solution)/shard_map/all_to_all | solution.py:67
  283.0 187.1 %all-to-all-start.2 = ((bf16[64,2,2,1024]{3,2,1,0:T(2,128)(2,1)}), bf16[64,2,2,1024]{3,2,1,0:T(2,128)(2,1)S(1)}, u32[]{:S(2)}, u32[]{:S(2)}) async-start(bf16[64,2,2,1024]{3,2,1,0:T(2,128)(2,1)} %copy.52), calls=%async_computation.2 | async-start | bytes 1048576 | tf_op jit(solution)/shard_map/all_to_all | solution.py:50
  288.4 180.3 %all-reduce.3.cloned.1.call-start = ((), (), s32[]{:S(2)}) async-start(), calls=%async_computation.7 | async-start | bytes 524288
  317.5 245.8 %reduce-scatter.4.cloned.1.call-start = ((), (), s32[]{:S(2)}) async-start(), calls=%async_computation.6 | async-start | bytes 278528
Sparse Core Ops, SparseCore 0:
  317.6 151.0 all-reduce.2
  473.9 89.3 reduce-scatter.3
